TPU v7x, 512 devices: a whole 4x4x16 slice. The times are simulated.
512 devices in a mesh: user: 32 (over x, y, core), item: 16 (over z).
Axes of the slice: x: 4, y: 4, z: 16, core: 2. Of those that a mesh axis runs over, the one named last changes fastest.
Arguments:
- tokens: bfloat16 [262144, 1024], P(('user', 'item')), may hold values from -6 to 6
- lengths: int32 [512, 32], P(('user', 'item')), may hold values from 1 to 16, as said below
- destination: int32 [512, 32], P(('user', 'item')), may hold values from 0 to 31, as said below
- worker_offset: int32 [512, 32], P(('user', 'item')), may hold values from 0 to 255
- positives: int32 [262144], P(('user', 'item')), may hold values from 0 to 4095, as said below
- negatives: int32 [16, 256], replicated, may hold values from 0 to 4095, as said below
- table: bfloat16 [4096, 1024], P('item'), may hold values from -6 to 6
- in_gain: float32 [1024], replicated, may hold values from 0.1 to 1.9
- w_uvqk: bfloat16 [1024, 2048], P('item'), may hold values from -0.1875 to 0.1875
- out_gain: float32 [512], replicated, may hold values from 0.1 to 1.9
- w_out: bfloat16 [512, 1024], P(None, 'item'), may hold values from -0.25 to 0.25
Outputs:
- layer_out: bfloat16 [131072, 1024], P(('user', 'item'))
- token_grad: bfloat16 [262144, 1024], P(('user', 'item'))
- item_grad: float32 [4096, 1024], P('item', 'user')
Inputs may be any that keep to these rules, and one draw needn't show every extreme that they name: `lengths`: A device's histories lie in its rows in order from row 0 and fill at most 512 rows; every destination receives a history of exactly 16 tokens. `destination`: A device sends its 32 histories to 32 different destinations along user; the histories sent to one device by the devices of its item index, placed at their worker_offset, cover its 256 rows exactly once. `positives`: the target ids of a device lie among the 256 table rows of its item index. `negatives`: columns k * 16 to k * 16 + 15 of each group name rows held by item index k.
All inputs are finite; a program needn't handle non-finite values.
Results may differ from a plain program's by a relative error of at most 0.017.
Values may be sent and summed in bfloat16 or wider, within the bound.
No kernel may reach another device: no remote copies, remote signals or barrier semaphores. Data moves between devices by JAX's collectives and lax.ppermute only.
A program may use at most 64 MiB of HBM per device.

v0:
```python
import jax
import jax.numpy as jnp
from jax import lax
from jax.sharding import PartitionSpec as P

HEAD = 128
TOK_DEV = 256
norm_epsilon = 1e-05
scale_epsilon = 1e-06
inverse_temp = 20.0
loss_scale = 32.0


def joined_along(blocks, dim):
    blocks = jnp.moveaxis(blocks, 0, dim)
    shape = blocks.shape
    return blocks.reshape(*shape[:dim], shape[dim] * shape[dim + 1], *shape[dim + 2 :])


def from_everyone(shard, axis):
    count = lax.axis_size(axis)
    return lax.all_to_all(
        jnp.broadcast_to(shard[None], (count, *shard.shape)), axis, 0, 0, tiled=True
    )


def gather_directly(shard, axis, dim):
    return joined_along(from_everyone(shard, axis), dim)


def in_blocks(shard, dim, count):
    shape = shard.shape
    blocks = shard.reshape(*shape[:dim], count, shape[dim] // count, *shape[dim + 1 :])
    return jnp.moveaxis(blocks, dim, 0)


def sent_and_summed(shard, axis, dim):
    count = lax.axis_size(axis)
    blocks = lax.all_to_all(in_blocks(shard, dim, count), axis, 0, 0, tiled=True)
    return jnp.sum(blocks.astype(jnp.float32), axis=0)


def over_copies(shard, axis):
    everything = from_everyone(shard, axis)
    return jnp.sum(everything, axis=0)


def layer_norm(values, gain):
    center = jnp.mean(values, axis=-1, keepdims=True)
    shifted = values - center
    spread = jnp.mean(shifted * shifted, axis=-1, keepdims=True)
    return shifted * lax.rsqrt(spread + norm_epsilon) * gain


def hstu_block(rows, segment, in_gain, w_uvqk, out_gain, w_out):
    count = rows.shape[0]
    rows_f = rows.astype(jnp.float32)
    normed = layer_norm(rows_f, in_gain).astype(jnp.bfloat16)
    projected = jnp.dot(
        normed,
        lax.all_gather(w_uvqk, "item", axis=0, tiled=True),
        preferred_element_type=jnp.float32,
    )
    active = jax.nn.silu(projected).astype(jnp.bfloat16)
    width = active.shape[1] // 4
    heads = width // HEAD
    gate_u = active[:, :width]
    values_v = active[:, width : 2 * width].reshape(count, heads, HEAD)
    queries = active[:, 2 * width : 3 * width].reshape(count, heads, HEAD)
    key_rows = active[:, 3 * width :].reshape(count, heads, HEAD)
    scores = jnp.einsum(
        "qhd,khd->hqk", queries, key_rows, preferred_element_type=jnp.float32
    ) * HEAD ** (-0.5)
    order = jnp.arange(count, dtype=jnp.int32)
    allowed = (segment[:, None] == segment[None, :]) & (order[None, :] <= order[:, None])
    weights = jnp.where(allowed[None], jax.nn.silu(scores), 0.0).astype(jnp.bfloat16)
    mixed = jnp.einsum(
        "hqk,khd->qhd", weights, values_v, preferred_element_type=jnp.float32
    ).reshape(count, width)
    gated = (layer_norm(mixed, out_gain) * gate_u.astype(jnp.float32)).astype(jnp.bfloat16)
    delta = jnp.dot(gated, gather_directly(w_out, "item", 1), preferred_element_type=jnp.float32)
    return (rows_f + delta).astype(jnp.bfloat16)


def dispatch(rows, home_start, history_len, targets, offsets, slot_rows, user_count):
    peers = jnp.arange(user_count, dtype=jnp.int32)
    chosen = (targets[None, :] == peers[:, None]).astype(jnp.int32)
    first_row = jnp.sum(chosen * home_start[None, :], axis=1)
    sent_count = jnp.sum(chosen * history_len[None, :], axis=1)
    landing = jnp.sum(chosen * offsets[None, :], axis=1)
    within = jnp.arange(slot_rows, dtype=jnp.int32)
    picked = jnp.minimum(first_row[:, None] + within[None, :], rows.shape[0] - 1)
    filled = within[None, :] < sent_count[:, None]
    parcels = jnp.where(filled[:, :, None], rows[picked], jnp.zeros((), rows.dtype))
    labels = jnp.stack([landing, sent_count], axis=1)
    arrived, arrived_labels = (
        lax.all_to_all(parcels, "user", split_axis=0, concat_axis=0, tiled=True),
        lax.all_to_all(labels, "user", split_axis=0, concat_axis=0, tiled=True),
    )
    worker_rows = jnp.arange(TOK_DEV, dtype=jnp.int32)
    lower = arrived_labels[:, 0]
    upper = lower + arrived_labels[:, 1]
    inside = (
        (worker_rows[:, None] >= lower[None, :]) & (worker_rows[:, None] < upper[None, :])
    ).astype(jnp.int32)
    source = jnp.sum(inside * peers[None, :], axis=1)
    begin = jnp.sum(inside * lower[None, :], axis=1)
    flattened = arrived.reshape(-1, arrived.shape[-1])
    gathered = flattened[source * slot_rows + worker_rows - begin]
    return (gathered, source, arrived_labels)


def per_device(
    tokens,
    lengths,
    destination,
    worker_offset,
    positives,
    negatives,
    table,
    in_gain,
    w_uvqk,
    out_gain,
    w_out,
):
    user_count = lax.axis_size("user")
    item_count = lax.axis_size("item")
    item_here = lax.axis_index("item")
    user_here = lax.axis_index("user")
    home_rows = tokens.shape[0]
    model_width = tokens.shape[1]
    hist_count = lengths.shape[1]
    slot_rows = home_rows // hist_count
    history_len = lengths[0]
    targets = destination[0]
    offsets = worker_offset[0]
    home_start = jnp.cumsum(history_len) - history_len
    row_ids = jnp.arange(home_rows, dtype=jnp.int32)
    finished = (row_ids[:, None] >= (home_start + history_len)[None, :]).astype(jnp.int32)
    home_segment = jnp.sum(finished, axis=1)
    valid = row_ids < jnp.sum(history_len)
    home_out = hstu_block(tokens, home_segment, in_gain, w_uvqk, out_gain, w_out)
    layer_out = dispatch(
        home_out, home_start, history_len, targets, offsets, slot_rows, user_count
    )[0]
    item_rows = table.shape[0]
    table_f = table.astype(jnp.float32)
    table_scale = lax.rsqrt(jnp.mean(table_f * table_f, axis=1) + scale_epsilon)
    table_hat = table_f * table_scale[:, None]
    table_low = table_hat.astype(jnp.bfloat16)
    share = negatives.shape[1] // item_count
    owned_ids = (
        lax.dynamic_slice_in_dim(negatives, item_here * share, share, 1) - item_here * item_rows
    )
    group_rows = lax.all_to_all(
        table_low[owned_ids], "item", split_axis=0, concat_axis=0, tiled=True
    ).reshape(-1, model_width)
    positive_local = positives - item_here * item_rows
    positive_rows = table_low[positive_local]
    out_f = home_out.astype(jnp.float32)
    out_scale = lax.rsqrt(jnp.mean(out_f * out_f, axis=1) + scale_epsilon)
    out_hat = out_f * out_scale[:, None]
    out_low = out_hat.astype(jnp.bfloat16)
    factor = inverse_temp / model_width
    positive_logit = (
        jnp.einsum("rd,rd->r", out_low, positive_rows, preferred_element_type=jnp.float32) * factor
    )
    negative_logit = (
        jnp.einsum("rd,nd->rn", out_low, group_rows, preferred_element_type=jnp.float32) * factor
    )
    positive_exp = jnp.exp(positive_logit)
    negative_exp = jnp.exp(negative_logit)
    partition = positive_exp + jnp.sum(negative_exp, axis=1)
    weight = jnp.where(valid, loss_scale, 0.0)
    positive_grad = weight * (positive_exp / partition - 1.0)
    negative_grad = (weight[:, None] * negative_exp / partition[:, None]).astype(jnp.bfloat16)
    grad_hat = (
        positive_grad[:, None] * positive_rows.astype(jnp.float32)
        + jnp.dot(negative_grad, group_rows, preferred_element_type=jnp.float32)
    ) * factor
    token_grad = (
        (grad_hat - out_hat * jnp.mean(grad_hat * out_hat, axis=1, keepdims=True))
        * out_scale[:, None]
    ).astype(jnp.bfloat16)
    negative_terms = (
        jnp.einsum("rn,rd->nd", negative_grad, out_low, preferred_element_type=jnp.float32) * factor
    )
    owned_terms = lax.all_to_all(
        negative_terms.reshape(item_count, share, model_width).astype(jnp.bfloat16),
        "item",
        split_axis=0,
        concat_axis=0,
        tiled=True,
    ).astype(jnp.float32)
    positive_terms = (positive_grad * factor)[:, None] * out_low.astype(jnp.float32)
    catalog = jnp.arange(item_rows, dtype=jnp.int32)
    positive_hits = (positive_local[None, :] == catalog[:, None]).astype(jnp.float32)
    negative_hits = (owned_ids.reshape(-1)[None, :] == catalog[:, None]).astype(jnp.float32)
    row_sums = jnp.dot(positive_hits, positive_terms)
    row_sums = row_sums + jnp.dot(negative_hits, owned_terms.reshape(-1, model_width))
    column_width = model_width // user_count
    part = sent_and_summed(row_sums.astype(jnp.bfloat16), "user", 1)
    hat_part = lax.dynamic_slice_in_dim(table_hat, user_here * column_width, column_width, 1)
    inner = over_copies(jnp.sum(part * hat_part, axis=1), "user") / model_width
    item_grad = (part - hat_part * inner[:, None]) * table_scale[:, None]
    return (layer_out, token_grad, item_grad)


def solution(mesh):
    return jax.shard_map(
        per_device,
        mesh=mesh,
        in_specs=(
            P(("user", "item"), None),
            P(("user", "item"), None),
            P(("user", "item"), None),
            P(("user", "item"), None),
            P(("user", "item")),
            P(),
            P("item", None),
            P(),
            P("item", None),
            P(),
            P(None, "item"),
        ),
        out_specs=(P(("user", "item"), None), P(("user", "item"), None), P("item", "user")),
        check_vma=False,
    )
```

profile of v0, /device:TPU:1, one launch (start us, length us, event | category | flops | bytes accessed | tf_op | source)
XLA Modules:
  0.0 277.3 jit_solution(9776412261107728501)
XLA Ops:
  7.3 0.7 all-gather.2.cloned.1.call-update
  7.9 1.9 broadcast_in_dim.43
  9.9 15.8 %all-to-all-start = ((bf16[16,512,64]{1,2,0:T(8,128)(2,1)}), bf16[16,512,64]{1,2,0:T(8,128)(2,1)}, u32[]{:S(2)}, u32[]{:S(2)}) async-start(bf16[16,512,64]{1,2,0:T(8,128)(2,1)} %broadcast_in_dim.43), calls=%async_computation | async-start | bytes 2097152 | tf_op jit(solution)/shard_map/all_to_all | solution.py:22
  25.7 0.1 copy.50
  25.8 0.1 reduce.6
  25.9 0.1 compare_select_fusion.1
  26.0 0.1 reshape.292
  26.1 0.2 fusion.23
  26.3 1.2 convert_multiply_fusion.8
  27.5 2.0 gather_fusion.2
  29.6 2.0 gather_fusion.3
  31.6 0.7 fusion.61
  32.3 0.1 select_reduce_fusion.2
  32.4 0.7 copy.55
  33.1 0.7 fusion.51
  33.8 0.1 convert_reduce_fusion.2
  33.9 0.2 convert_reduce_fusion
  34.1 0.4 fusion.5
  34.6 0.2 fusion.34
  34.8 87.9 %all-gather.2.cloned.1.call-done = bf16[1024,2048]{1,0:T(8,128)(2,1)} async-done(((bf16[64,2048]{1,0:T(8,128)(2,1)}), bf16[1024,2048]{1,0:T(8,128)(2,1)}) %all-gather.2.cloned.1.call-update) | async-done | bytes 4194320 | tf_op jit(solution)/shard_map/all_gather | solution.py:61
  122.7 5.1 %multiply_convert_fusion = bf16[512,2048]{1,0:T(8,128)(2,1)S(1)} fusion(bf16[1024,2048]{1,0:T(8,128)(2,1)} %all-gather.2.cloned.1.call-done, bf16[512,1024]{1,0:T(8,128)(2,1)S(1)} %copy-done, f32[1024]{0:T(1024)S(1)} %copy-done.8, f32[512]{0:T(512)S(1)} %add_rsqrt_fusion.2, f32[512]{0:T(512)S(1)} %broadcast_multiply_fusion.3), kind=kOutput, calls=%fused_computation.5 | convolution fusion | flops 2155347968 | bytes 7348224 | tf_op jit(solution)/shard_map/dot_general | solution.py:59
  127.7 1.3 copy-done.2
  129.1 1.2 slice_bitcast_fusion.1
  130.3 1.0 copy.66
  131.3 7.0 %all-to-all-start.3 = ((bf16[16,16,1024]{2,1,0:T(8,128)(2,1)}), bf16[16,16,1024]{2,1,0:T(8,128)(2,1)}, u32[]{:S(2)}, u32[]{:S(2)}) async-start(bf16[16,16,1024]{2,1,0:T(8,128)(2,1)} %bitcast.21), calls=%async_computation.3 | async-start | bytes 1048576 | tf_op jit(solution)/shard_map/all_to_all | solution.py:155
  138.3 3.4 %fusion.62 = (f32[512]{0:T(512)S(1)}, f32[4,128,512]{2,1,0:T(8,128)S(1)}) fusion(bf16[512,4,128]{0,2,1:T(8,128)(2,1)} %bitcast.73, pred[512,512]{1,0:T(8,128)(4,1)S(1)} %fusion.34, bf16[64,4,8,128]{3,2,1,0:T(8,128)(2,1)} %get-tuple-element.30, bf16[64,4,8,128]{3,2,1,0:T(8,128)(2,1)} %get-tuple-element.29), kind=kOutput, calls=%fused_computation.120 | convolution fusion | flops 544472576 | bytes 2885632 | tf_op jit(solution)/shard_map/hqk,khd->qhd/dot_general | solution.py:77
  141.7 1.3 copy.67
  143.0 0.2 fusion.29
  143.2 2.6 fusion.12
  145.8 0.5 fusion.15
  146.3 10.5 %all-to-all-done.3 = bf16[16,16,1024]{2,1,0:T(8,128)(2,1)} async-done(((bf16[16,16,1024]{2,1,0:T(8,128)(2,1)}), bf16[16,16,1024]{2,1,0:T(8,128)(2,1)}, u32[]{:S(2)}, u32[]{:S(2)}) %all-to-all-start.3) | async-done | bytes 524320 | tf_op jit(solution)/shard_map/all_to_all | solution.py:155
  156.8 17.8 %all-to-all-start.2 = ((s32[32,1,2]{2,1,0:T(1,128)}), s32[32,1,2]{2,1,0:T(1,128)S(1)}, u32[]{:S(2)}, u32[]{:S(2)}) async-start(s32[32,1,2]{2,1,0:T(1,128)} %copy.55), calls=%async_computation.2 | async-start | bytes 32768 | tf_op jit(solution)/shard_map/all_to_all | solution.py:98
  174.7 1.6 fusion.67
  176.3 0.7 broadcast_multiply_fusion
  177.0 1.4 fusion.20
  178.4 3.2 %all-to-all-done.2 = s32[32,1,2]{2,1,0:T(1,128)S(1)} async-done(((s32[32,1,2]{2,1,0:T(1,128)}), s32[32,1,2]{2,1,0:T(1,128)S(1)}, u32[]{:S(2)}, u32[]{:S(2)}) %all-to-all-start.2) | async-done | bytes 288 | tf_op jit(solution)/shard_map/all_to_all | solution.py:98
  181.6 6.8 %all-to-all-start.4 = ((bf16[16,16,1024]{2,1,0:T(8,128)(2,1)}), bf16[16,16,1024]{2,1,0:T(8,128)(2,1)S(1)}, u32[]{:S(2)}, u32[]{:S(2)}) async-start(bf16[16,16,1024]{2,1,0:T(8,128)(2,1)} %bitcast.23), calls=%async_computation.4 | async-start | bytes 1048576 | tf_op jit(solution)/shard_map/all_to_all | solution.py:188
  188.4 0.1 eq.70
  188.5 0.1 compare_select_fusion
  188.5 0.1 reshape.268
  188.6 0.1 iota_compare_fusion.9
  188.7 0.1 copy.56
  188.8 22.6 %all-to-all-done.4 = bf16[16,16,1024]{2,1,0:T(8,128)(2,1)S(1)} async-done(((bf16[16,16,1024]{2,1,0:T(8,128)(2,1)}), bf16[16,16,1024]{2,1,0:T(8,128)(2,1)S(1)}, u32[]{:S(2)}, u32[]{:S(2)}) %all-to-all-start.4) | async-done | bytes 524320 | tf_op jit(solution)/shard_map/all_to_all | solution.py:188
  211.4 0.3 fusion.48
  211.7 0.6 fusion.21
  212.3 1.0 copy.57
  213.3 11.2 %all-to-all-start.5 = ((bf16[32,256,32]{1,2,0:T(8,128)(2,1)}), bf16[32,256,32]{1,2,0:T(8,128)(2,1)}, u32[]{:S(2)}, u32[]{:S(2)}) async-start(bf16[32,256,32]{1,2,0:T(8,128)(2,1)} %bitcast.26), calls=%async_computation.5 | async-start | bytes 1048576 | tf_op jit(solution)/shard_map/all_to_all | solution.py:39
  224.6 0.1 select_reduce_fusion.1
  224.7 2.1 gather_fusion
  226.7 1.1 broadcast_select_fusion
  227.8 8.5 %all-to-all-done.5 = bf16[32,256,32]{1,2,0:T(8,128)(2,1)} async-done(((bf16[32,256,32]{1,2,0:T(8,128)(2,1)}), bf16[32,256,32]{1,2,0:T(8,128)(2,1)}, u32[]{:S(2)}, u32[]{:S(2)}) %all-to-all-start.5) | async-done | bytes 524320 | tf_op jit(solution)/shard_map/all_to_all | solution.py:39
  236.3 3.7 %all-to-all-start.1 = ((bf16[32,16,1024]{2,1,0:T(8,128)(2,1)}), bf16[32,16,1024]{2,1,0:T(8,128)(2,1)S(1)}, u32[]{:S(2)}, u32[]{:S(2)}) async-start(bf16[32,16,1024]{2,1,0:T(8,128)(2,1)} %broadcast_select_fusion), calls=%async_computation.1 | async-start | bytes 2097152 | tf_op jit(solution)/shard_map/all_to_all | solution.py:97
  240.1 3.3 %fusion.8 = (f32[512]{0:T(512)S(1)}, f32[512,1024]{1,0:T(8,128)}) fusion(bf16[512,1024]{1,0:T(8,128)(2,1)S(1)} %get-tuple-element.40, f32[512]{0:T(512)S(1)} %add_rsqrt_fusion, bf16[256,1024]{1,0:T(8,128)(2,1)} %bitcast.22, f32[512,256]{0,1:T(8,128)} %copy-done.10, f32[512]{0:T(512)S(1)} %get-tuple-element.34, f32[512]{0:T(512)S(1)} %fusion.51, ...), kind=kOutput, calls=%fused_computation.22 | convolution fusion | flops 273022464 | bytes 5253120 | tf_op jit(solution)/shard_map/dot_general | solution.py:179
  243.4 1.1 convert_reduce_fusion.1
  244.5 0.1 copy.60
  244.6 1.1 multiply_reduce_fusion
  245.7 11.1 %all-to-all-done.1 = bf16[32,16,1024]{2,1,0:T(8,128)(2,1)S(1)} async-done(((bf16[32,16,1024]{2,1,0:T(8,128)(2,1)}), bf16[32,16,1024]{2,1,0:T(8,128)(2,1)S(1)}, u32[]{:S(2)}, u32[]{:S(2)}) %all-to-all-start.1) | async-done | bytes 1048608 | tf_op jit(solution)/shard_map/all_to_all | solution.py:97
  256.8 0.6 broadcast_in_dim.50
  257.4 3.9 %all-to-all-start.6 = ((f32[32,1,256]{2,1,0:T(1,128)}), f32[32,1,256]{2,1,0:T(1,128)S(1)}, u32[]{:S(2)}, u32[]{:S(2)}) async-start(f32[32,1,256]{2,1,0:T(1,128)} %broadcast_in_dim.50), calls=%async_computation.6 | async-start | bytes 65536 | tf_op jit(solution)/shard_map/all_to_all | solution.py:22
  261.4 3.0 %fusion.11 = bf16[512,1024]{1,0:T(8,128)(2,1)} fusion(f32[512,1024]{1,0:T(8,128)} %get-tuple-element.44, bf16[512,1024]{1,0:T(8,128)(2,1)S(1)} %get-tuple-element.40, f32[512]{0:T(512)S(1)} %broadcast_multiply_fusion.2, f32[512]{0:T(512)S(1)} %add_rsqrt_fusion), kind=kLoop, calls=%fused_computation.25 | loop fusion | flops 3145728 | bytes 4198400 | tf_op jit(solution)/shard_map/convert_element_type | solution.py:184
  264.4 2.0 gather_fusion.1
  266.3 2.3 all-to-all-done.6
  268.7 1.1 subtract_multiply_fusion
  269.8 0.7 copy.61
  (43 shorter events, 0.3 us)
Async XLA Ops:
  7.2 18.5 %copy-start.3 = (s32[1,32]{1,0:T(1,128)S(1)}, s32[1,32]{1,0:T(1,128)}, u32[]{:S(2)}) copy-start(s32[1,32]{1,0:T(1,128)} %param.12) | copy-start | bytes 388
  7.2 18.7 %copy-start.4 = (s32[16,256]{1,0:T(8,128)S(1)}, s32[16,256]{1,0:T(8,128)}, u32[]{:S(2)}) copy-start(s32[16,256]{1,0:T(8,128)} %param.16) | copy-start | bytes 49156
  7.2 18.9 %copy-start.5 = (s32[512]{0:T(512)S(1)}, s32[512]{0:T(512)}, u32[]{:S(2)}) copy-start(s32[512]{0:T(512)} %param.15) | copy-start | bytes 6148
  7.2 18.9 %copy-start.1 = (bf16[256,1024]{1,0:T(8,128)(2,1)S(1)}, bf16[256,1024]{1,0:T(8,128)(2,1)}, u32[]{:S(2)}) copy-start(bf16[256,1024]{1,0:T(8,128)(2,1)} %param.17) | copy-start | bytes 1572868
  7.2 115.4 %all-gather.2.cloned.1.call-start = ((), (), s32[]{:S(2)}) async-start(), calls=%async_computation.7 | async-start | bytes 4456448 | tf_op jit(solution)/shard_map/all_gather | solution.py:61
  9.9 121.4 %all-to-all-start = ((bf16[16,512,64]{1,2,0:T(8,128)(2,1)}), bf16[16,512,64]{1,2,0:T(8,128)(2,1)}, u32[]{:S(2)}, u32[]{:S(2)}) async-start(bf16[16,512,64]{1,2,0:T(8,128)(2,1)} %broadcast_in_dim.43), calls=%async_computation | async-start | bytes 2097152 | tf_op jit(solution)/shard_map/all_to_all | solution.py:22
  29.5 2.7 copy-start.6
  29.6 2.7 copy-start.7
  29.6 4.4 %copy-start = (bf16[512,1024]{1,0:T(8,128)(2,1)S(1)}, bf16[512,1024]{1,0:T(8,128)(2,1)}, u32[]{:S(2)}) copy-start(bf16[512,1024]{1,0:T(8,128)(2,1)} %param.11) | copy-start | bytes 3145732
  31.6 91.1 %copy-start.8 = (f32[1024]{0:T(1024)S(1)}, f32[1024]{0:T(1024)}, u32[]{:S(2)}) copy-start(f32[1024]{0:T(1024)} %param.18) | copy-start | bytes 12292
  127.7 1.4 copy-start.2
  131.3 25.5 %all-to-all-start.3 = ((bf16[16,16,1024]{2,1,0:T(8,128)(2,1)}), bf16[16,16,1024]{2,1,0:T(8,128)(2,1)}, u32[]{:S(2)}, u32[]{:S(2)}) async-start(bf16[16,16,1024]{2,1,0:T(8,128)(2,1)} %bitcast.21), calls=%async_computation.3 | async-start | bytes 1048576 | tf_op jit(solution)/shard_map/all_to_all | solution.py:155
  141.7 1.5 copy-start.9
  156.8 24.8 %all-to-all-start.2 = ((s32[32,1,2]{2,1,0:T(1,128)}), s32[32,1,2]{2,1,0:T(1,128)S(1)}, u32[]{:S(2)}, u32[]{:S(2)}) async-start(s32[32,1,2]{2,1,0:T(1,128)} %copy.55), calls=%async_computation.2 | async-start | bytes 32768 | tf_op jit(solution)/shard_map/all_to_all | solution.py:98
  176.3 5.3 %copy-start.10 = (f32[512,256]{0,1:T(8,128)}, f32[512,256]{0,1:T(8,128)S(1)}, u32[]{:S(2)}) copy-start(f32[512,256]{0,1:T(8,128)S(1)} %get-tuple-element.42) | copy-start | bytes 1572868
  181.6 29.8 %all-to-all-start.4 = ((bf16[16,16,1024]{2,1,0:T(8,128)(2,1)}), bf16[16,16,1024]{2,1,0:T(8,128)(2,1)S(1)}, u32[]{:S(2)}, u32[]{:S(2)}) async-start(bf16[16,16,1024]{2,1,0:T(8,128)(2,1)} %bitcast.23), calls=%async_computation.4 | async-start | bytes 1048576 | tf_op jit(solution)/shard_map/all_to_all | solution.py:188
  213.3 23.0 %all-to-all-start.5 = ((bf16[32,256,32]{1,2,0:T(8,128)(2,1)}), bf16[32,256,32]{1,2,0:T(8,128)(2,1)}, u32[]{:S(2)}, u32[]{:S(2)}) async-start(bf16[32,256,32]{1,2,0:T(8,128)(2,1)} %bitcast.26), calls=%async_computation.5 | async-start | bytes 1048576 | tf_op jit(solution)/shard_map/all_to_all | solution.py:39
  236.3 20.5 %all-to-all-start.1 = ((bf16[32,16,1024]{2,1,0:T(8,128)(2,1)}), bf16[32,16,1024]{2,1,0:T(8,128)(2,1)S(1)}, u32[]{:S(2)}, u32[]{:S(2)}) async-start(bf16[32,16,1024]{2,1,0:T(8,128)(2,1)} %broadcast_select_fusion), calls=%async_computation.1 | async-start | bytes 2097152 | tf_op jit(solution)/shard_map/all_to_all | solution.py:97
  257.4 11.2 %all-to-all-start.6 = ((f32[32,1,256]{2,1,0:T(1,128)}), f32[32,1,256]{2,1,0:T(1,128)S(1)}, u32[]{:S(2)}, u32[]{:S(2)}) async-start(f32[32,1,256]{2,1,0:T(1,128)} %broadcast_in_dim.50), calls=%async_computation.6 | async-start | bytes 65536 | tf_op jit(solution)/shard_map/all_to_all | solution.py:22
Sparse Core Ops, SparseCore 0:
  10.1 112.5 all-gather.1
where the time goes:
time: 278 us; the launch traced here: 277 us
  waiting for transfers between devices  147 us (53%)
  starting transfers between devices  66.3 us (24%)
  local copies, waits for them, and re-layouts  18.4 us (7%)
  matrix products  18.3 us (7%)
  between operations  14.4 us (5%)
  other arithmetic  13.3 us (5%)
    all_gather x1, waiting for transfers between devices, hstu_block(): lax.all_gather(w_uvqk, 'item', axis=0, tiled=True)  87.9 us
    all_to_all x1, waiting for transfers between devices, per_device(): lax.all_to_all(negative_terms.reshape(item_count, share, model_width).ast...  22.6 us
    all_to_all x2, starting transfers between devices, from_everyone(): lax.all_to_all(jnp.broadcast_to(shard[None], (count, *shard.shape)), axis...  19.7 us
    all_to_all x1, starting transfers between devices, dispatch(): lax.all_to_all(labels, 'user', split_axis=0, concat_axis=0, tiled=True)  17.8 us
    all_to_all x1, starting transfers between devices, sent_and_summed(): lax.all_to_all(in_blocks(shard, dim, count), axis, 0, 0, tiled=True)  11.2 us
    all_to_all x1, waiting for transfers between devices, dispatch(): lax.all_to_all(parcels, 'user', split_axis=0, concat_axis=0, tiled=True)  11.1 us
    all_to_all x1, waiting for transfers between devices, per_device(): lax.all_to_all(table_low[owned_ids], 'item', split_axis=0, concat_axis=0,...  10.5 us
    all_to_all x1, waiting for transfers between devices, sent_and_summed(): lax.all_to_all(in_blocks(shard, dim, count), axis, 0, 0, tiled=True)  8.47 us
  transfers between devices with their start and end apart: 8, of which 7 were waited for; matrix products, arithmetic and copies ran while one was open for 16% of the time, Pallas kernels for 0%

commit v1 on v0

--- a/solution.py
+++ b/solution.py
@@ -11,6 +11,34 @@
 loss_scale = 32.0
 
 
+def _push_records(view, mesh_ax):
+    near = jax.lax.axis_size(mesh_ax)
+    y2, base_arr, res = (near, jax.lax.axis_index(mesh_ax), view.shape[0])
+    found = []
+    for d, u in enumerate(view.shape):
+        found.append(u * y2 if d == 0 else u)
+    z = jnp.zeros(found, view.dtype)
+    part_now = lax.dynamic_update_slice_in_dim(z, view, base_arr * res, axis=0)
+    z_new = next_value = view
+    for pp in range(1, y2 // 2 + 1):
+        row_list = []
+        for d in range(y2):
+            row_list.append((d, (d + 1) % y2))
+        z_new = jax.lax.ppermute(z_new, mesh_ax, perm=row_list)
+        part_now = lax.dynamic_update_slice_in_dim(
+            part_now, z_new, (base_arr - pp) % y2 * res, axis=0
+        )
+        if 2 * pp < y2:
+            crops = []
+            for d in range(y2):
+                crops.append((d, (d - 1) % y2))
+            next_value = jax.lax.ppermute(next_value, mesh_ax, perm=crops)
+            part_now = lax.dynamic_update_slice_in_dim(
+                part_now, next_value, (base_arr + pp) % y2 * res, axis=0
+            )
+    return part_now
+
+
 def joined_along(blocks, dim):
     blocks = jnp.moveaxis(blocks, 0, dim)
     shape = blocks.shape
@@ -57,9 +85,7 @@
     rows_f = rows.astype(jnp.float32)
     normed = layer_norm(rows_f, in_gain).astype(jnp.bfloat16)
     projected = jnp.dot(
-        normed,
-        lax.all_gather(w_uvqk, "item", axis=0, tiled=True),
-        preferred_element_type=jnp.float32,
+        normed, _push_records(w_uvqk, mesh_ax="item"), preferred_element_type=jnp.float32
     )
     active = jax.nn.silu(projected).astype(jnp.bfloat16)
     width = active.shape[1] // 4

time: 278 us -> 287 us (1.032)
  starting transfers between devices: 66.3 us -> 118 us
  waiting for transfers between devices: 147 us -> 96.1 us
  local copies, waits for them, and re-layouts: 18.4 us -> 35.1 us
  between operations: 14.4 us -> 1.38 us
    all_gather x1 -> x0, waiting for transfers between devices: 87.9 us -> none  [hstu_block(): lax.all_gather(w_uvqk, 'item', axis=0, tiled=True)]
    ppermute x0 -> x15, starting transfers between devices: none -> 54.8 us  [the longest x7 35.6 us: _push_records(): next_value = jax.lax.ppermute(next_value, mesh_ax, perm=crops)]
    ppermute x0 -> x15, waiting for transfers between devices: none -> 37.4 us  [the longest x8 37.4 us: _push_records(): z_new = jax.lax.ppermute(z_new, mesh_ax, perm=row_list)]
    dynamic_update_slice x0 -> x16, local copies, waits for them, and re-layouts: none -> 13.5 us  [the longest x8 6.81 us: _push_records(): lax.dynamic_update_slice_in_dim(part_now, z_new, (base_arr - pp) % y2 * r...]
    all_to_all x2, starting transfers between devices: 19.7 us -> 12.3 us  [from_everyone(): lax.all_to_all(jnp.broadcast_to(shard[None], (count, *shard.shape)), axis...]
    all_to_all x1, starting transfers between devices: 6.96 us -> 11.9 us  [per_device(): lax.all_to_all(table_low[owned_ids], 'item', split_axis=0, concat_axis=0,...]
  transfers between devices with their start and end apart: 8 -> 22, of which waited for: 7 -> 13; matrix products, arithmetic and copies ran while one was open for 16% -> 23% of each run, Pallas kernels for 0% -> 0%
where the time goes in v1:
time: 287 us; the launch traced here: 285 us
  starting transfers between devices  118 us (41%)
  waiting for transfers between devices  96.1 us (33%)
  local copies, waits for them, and re-layouts  35.1 us (12%)
  matrix products  19.7 us (7%)
  other arithmetic  15 us (5%)
    ppermute x8, waiting for transfers between devices, _push_records(): z_new = jax.lax.ppermute(z_new, mesh_ax, perm=row_list)  37.4 us
    ppermute x7, starting transfers between devices, _push_records(): next_value = jax.lax.ppermute(next_value, mesh_ax, perm=crops)  35.6 us
    all_to_all x1, waiting for transfers between devices, per_device(): lax.all_to_all(negative_terms.reshape(item_count, share, model_width).ast...  22.6 us
    ppermute x8, starting transfers between devices, _push_records(): z_new = jax.lax.ppermute(z_new, mesh_ax, perm=row_list)  19.2 us
    all_to_all x1, starting transfers between devices, dispatch(): lax.all_to_all(labels, 'user', split_axis=0, concat_axis=0, tiled=True)  17.2 us
    all_to_all x2, starting transfers between devices, from_everyone(): lax.all_to_all(jnp.broadcast_to(shard[None], (count, *shard.shape)), axis...  12.3 us
    all_to_all x1, starting transfers between devices, per_device(): lax.all_to_all(table_low[owned_ids], 'item', split_axis=0, concat_axis=0,...  11.9 us
    all_to_all x1, starting transfers between devices, sent_and_summed(): lax.all_to_all(in_blocks(shard, dim, count), axis, 0, 0, tiled=True)  11.2 us
  transfers between devices with their start and end apart: 22, of which 13 were waited for; matrix products, arithmetic and copies ran while one was open for 23% of the time, Pallas kernels for 0%

profile of v1, /device:TPU:1, one launch (start us, length us, event | category | flops | bytes accessed | tf_op | source)
XLA Modules:
  0.0 285.4 jit_solution(17931109207435703850)
XLA Ops:
  0.7 4.5 %collective-permute-start = (bf16[64,2048]{1,0:T(8,128)(2,1)}, bf16[64,2048]{1,0:T(8,128)(2,1)}, u32[]{:S(2)}, u32[]{:S(2)}) collective-permute-start(bf16[64,2048]{1,0:T(8,128)(2,1)} %param.19), channel_id=1, source_target_pairs={{0,1},{1,2},{2,3},{3,4},{4,5},{5,6},{6,7},{7,8},{8,9},{9,10},{10,1... | collective-permute-start | bytes 786440 | tf_op jit(solution)/shard_map/ppermute | solution.py:27
  5.2 9.5 %collective-permute-start.1 = (bf16[64,2048]{1,0:T(8,128)(2,1)}, bf16[64,2048]{1,0:T(8,128)(2,1)}, u32[]{:S(2)}, u32[]{:S(2)}) collective-permute-start(bf16[64,2048]{1,0:T(8,128)(2,1)} %param.19), channel_id=1, source_target_pairs={{0,15},{1,0},{2,1},{3,2},{4,3},{5,4},{6,5},{7,6},{8,7},{9,8},{10,9... | collective-permute-start | bytes 786440 | tf_op jit(solution)/shard_map/ppermute | solution.py:35
  14.7 1.9 broadcast_in_dim.46
  16.6 8.4 %all-to-all-start = ((bf16[16,512,64]{1,2,0:T(8,128)(2,1)}), bf16[16,512,64]{1,2,0:T(8,128)(2,1)}, u32[]{:S(2)}, u32[]{:S(2)}) async-start(bf16[16,512,64]{1,2,0:T(8,128)(2,1)} %broadcast_in_dim.46), calls=%async_computation | async-start | bytes 2097152 | tf_op jit(solution)/shard_map/all_to_all | solution.py:50
  25.0 0.7 copy.50
  26.0 1.3 fusion.61
  27.4 1.4 convert_reduce_fusion
  29.5 1.2 convert_multiply_fusion.8
  31.5 2.5 broadcast_in_dim.43
  35.1 2.1 gather_fusion.2
  37.2 2.0 gather_fusion.3
  40.1 3.2 %collective-permute-start.2 = (bf16[64,2048]{1,0:T(8,128)(2,1)}, bf16[64,2048]{1,0:T(8,128)(2,1)S(1)}, u32[]{:S(2)}, u32[]{:S(2)}) collective-permute-start(bf16[64,2048]{1,0:T(8,128)(2,1)} %collective-permute-done), channel_id=1, source_target_pairs={{0,1},{1,2},{2,3},{3,4},{4,5},{5,6},{6,7},{7,8},{8,9},{9,10},{10,1... | collective-permute-start | bytes 786440 | tf_op jit(solution)/shard_map/ppermute | solution.py:27
  43.3 3.3 %collective-permute-start.3 = (bf16[64,2048]{1,0:T(8,128)(2,1)}, bf16[64,2048]{1,0:T(8,128)(2,1)S(1)}, u32[]{:S(2)}, u32[]{:S(2)}) collective-permute-start(bf16[64,2048]{1,0:T(8,128)(2,1)} %collective-permute-done.1), channel_id=1, source_target_pairs={{0,15},{1,0},{2,1},{3,2},{4,3},{5,4},{6,5},{7,6},{8,7},{9,8},{10,9... | collective-permute-start | bytes 786440 | tf_op jit(solution)/shard_map/ppermute | solution.py:35
  46.6 1.7 constant_dynamic-update-slice_fusion.14
  48.3 1.7 constant_dynamic-update-slice_fusion.13
  50.0 28.7 %collective-permute-done.2 = bf16[64,2048]{1,0:T(8,128)(2,1)S(1)} collective-permute-done((bf16[64,2048]{1,0:T(8,128)(2,1)}, bf16[64,2048]{1,0:T(8,128)(2,1)S(1)}, u32[]{:S(2)}, u32[]{:S(2)}) %collective-permute-start.2) | collective-permute-done | bytes 262176 | tf_op jit(solution)/shard_map/ppermute | solution.py:27
  78.6 1.9 collective-permute-start.4
  80.6 4.6 %collective-permute-start.5 = (bf16[64,2048]{1,0:T(8,128)(2,1)S(1)}, bf16[64,2048]{1,0:T(8,128)(2,1)S(1)}, u32[]{:S(2)}, u32[]{:S(2)}) collective-permute-start(bf16[64,2048]{1,0:T(8,128)(2,1)S(1)} %collective-permute-done.3), channel_id=1, source_target_pairs={{0,15},{1,0},{2,1},{3,2},{4,3},{5,4},{6,5},{7,6},{8,7},{9,8},{10,9... | collective-permute-start | bytes 786440 | tf_op jit(solution)/shard_map/ppermute | solution.py:35
  86.6 1.6 collective-permute-done.4
  88.2 1.9 collective-permute-start.6
  90.1 4.6 %collective-permute-start.7 = (bf16[64,2048]{1,0:T(8,128)(2,1)S(1)}, bf16[64,2048]{1,0:T(8,128)(2,1)S(1)}, u32[]{:S(2)}, u32[]{:S(2)}) collective-permute-start(bf16[64,2048]{1,0:T(8,128)(2,1)S(1)} %collective-permute-done.5), channel_id=1, source_target_pairs={{0,15},{1,0},{2,1},{3,2},{4,3},{5,4},{6,5},{7,6},{8,7},{9,8},{10,9... | collective-permute-start | bytes 786440 | tf_op jit(solution)/shard_map/ppermute | solution.py:35
  94.7 0.7 constant_dynamic-update-slice_fusion.10
  96.2 0.7 collective-permute-done.6
  96.9 1.9 collective-permute-start.8
  98.8 4.6 %collective-permute-start.9 = (bf16[64,2048]{1,0:T(8,128)(2,1)S(1)}, bf16[64,2048]{1,0:T(8,128)(2,1)S(1)}, u32[]{:S(2)}, u32[]{:S(2)}) collective-permute-start(bf16[64,2048]{1,0:T(8,128)(2,1)S(1)} %collective-permute-done.7), channel_id=1, source_target_pairs={{0,15},{1,0},{2,1},{3,2},{4,3},{5,4},{6,5},{7,6},{8,7},{9,8},{10,9... | collective-permute-start | bytes 786440 | tf_op jit(solution)/shard_map/ppermute | solution.py:35
  103.4 0.7 constant_dynamic-update-slice_fusion.8
  104.2 0.7 constant_dynamic-update-slice_fusion.7
  105.2 1.9 collective-permute-start.10
  107.2 4.6 %collective-permute-start.11 = (bf16[64,2048]{1,0:T(8,128)(2,1)S(1)}, bf16[64,2048]{1,0:T(8,128)(2,1)S(1)}, u32[]{:S(2)}, u32[]{:S(2)}) collective-permute-start(bf16[64,2048]{1,0:T(8,128)(2,1)S(1)} %collective-permute-done.9), channel_id=1, source_target_pairs={{0,15},{1,0},{2,1},{3,2},{4,3},{5,4},{6,5},{7,6},{8,7},{9,8},{10,9... | collective-permute-start | bytes 786440 | tf_op jit(solution)/shard_map/ppermute | solution.py:35
  111.7 0.7 constant_dynamic-update-slice_fusion.6
  113.6 1.9 collective-permute-start.12
  115.5 4.6 %collective-permute-start.13 = (bf16[64,2048]{1,0:T(8,128)(2,1)S(1)}, bf16[64,2048]{1,0:T(8,128)(2,1)S(1)}, u32[]{:S(2)}, u32[]{:S(2)}) collective-permute-start(bf16[64,2048]{1,0:T(8,128)(2,1)S(1)} %collective-permute-done.11), channel_id=1, source_target_pairs={{0,15},{1,0},{2,1},{3,2},{4,3},{5,4},{6,5},{7,6},{8,7},{9,8},{10,9... | collective-permute-start | bytes 786440 | tf_op jit(solution)/shard_map/ppermute | solution.py:35
  121.9 1.9 collective-permute-start.14
  125.2 5.3 %collective-permute-done.14 = bf16[64,2048]{1,0:T(8,128)(2,1)S(1)} collective-permute-done((bf16[64,2048]{1,0:T(8,128)(2,1)S(1)}, bf16[64,2048]{1,0:T(8,128)(2,1)S(1)}, u32[]{:S(2)}, u32[]{:S(2)}) %collective-permute-start.14) | collective-permute-done | bytes 262176 | tf_op jit(solution)/shard_map/ppermute | solution.py:27
  130.5 0.7 constant_dynamic-update-slice_fusion
  131.3 6.4 %multiply_convert_fusion = bf16[512,2048]{1,0:T(8,128)(2,1)} fusion(bf16[1024,2048]{1,0:T(8,128)(2,1)} %constant_dynamic-update-slice_fusion, bf16[512,1024]{1,0:T(8,128)(2,1)S(1)} %copy-done, f32[1024]{0:T(1024)S(1)} %copy-done.8, f32[512]{0:T(512)S(1)} %add_rsqrt_fusion.2, f32[512]{0:T(512)S(1)} %broadcast_multiply_fusion.3), kind=kOutput, calls=%fused_computation.5 | convolution fusion | flops 2155347968 | bytes 7348224 | tf_op jit(solution)/shard_map/dot_general | solution.py:87
  137.7 2.6 slice_bitcast_fusion.1
  140.3 1.0 copy.66
  141.3 11.9 %all-to-all-start.3 = ((bf16[16,16,1024]{2,1,0:T(8,128)(2,1)}), bf16[16,16,1024]{2,1,0:T(8,128)(2,1)}, u32[]{:S(2)}, u32[]{:S(2)}) async-start(bf16[16,16,1024]{2,1,0:T(8,128)(2,1)} %bitcast.21), calls=%async_computation.3 | async-start | bytes 1048576 | tf_op jit(solution)/shard_map/all_to_all | solution.py:181
  153.2 3.4 %fusion.62 = (f32[512]{0:T(512)S(1)}, f32[4,128,512]{2,1,0:T(8,128)S(1)}) fusion(bf16[512,4,128]{0,2,1:T(8,128)(2,1)} %bitcast.73, pred[512,512]{1,0:T(8,128)(4,1)S(1)} %fusion.34, bf16[64,4,8,128]{3,2,1,0:T(8,128)(2,1)} %get-tuple-element.30, bf16[64,4,8,128]{3,2,1,0:T(8,128)(2,1)} %get-tuple-element.29), kind=kOutput, calls=%fused_computation.136 | convolution fusion | flops 544472576 | bytes 2885632 | tf_op jit(solution)/shard_map/hqk,khd->qhd/dot_general | solution.py:103
  156.6 1.3 copy.67
  158.1 2.6 fusion.12
  161.2 11.0 %all-to-all-done.3 = bf16[16,16,1024]{2,1,0:T(8,128)(2,1)} async-done(((bf16[16,16,1024]{2,1,0:T(8,128)(2,1)}), bf16[16,16,1024]{2,1,0:T(8,128)(2,1)}, u32[]{:S(2)}, u32[]{:S(2)}) %all-to-all-start.3) | async-done | bytes 524320 | tf_op jit(solution)/shard_map/all_to_all | solution.py:181
  172.2 17.2 %all-to-all-start.2 = ((s32[32,1,2]{2,1,0:T(1,128)}), s32[32,1,2]{2,1,0:T(1,128)S(1)}, u32[]{:S(2)}, u32[]{:S(2)}) async-start(s32[32,1,2]{2,1,0:T(1,128)} %copy.55), calls=%async_computation.2 | async-start | bytes 32768 | tf_op jit(solution)/shard_map/all_to_all | solution.py:124
  189.4 1.6 fusion.67
  191.7 1.4 fusion.20
  193.1 3.2 %all-to-all-done.2 = s32[32,1,2]{2,1,0:T(1,128)S(1)} async-done(((s32[32,1,2]{2,1,0:T(1,128)}), s32[32,1,2]{2,1,0:T(1,128)S(1)}, u32[]{:S(2)}, u32[]{:S(2)}) %all-to-all-start.2) | async-done | bytes 288 | tf_op jit(solution)/shard_map/all_to_all | solution.py:124
  196.3 6.9 %all-to-all-start.4 = ((bf16[16,16,1024]{2,1,0:T(8,128)(2,1)}), bf16[16,16,1024]{2,1,0:T(8,128)(2,1)S(1)}, u32[]{:S(2)}, u32[]{:S(2)}) async-start(bf16[16,16,1024]{2,1,0:T(8,128)(2,1)} %bitcast.23), calls=%async_computation.4 | async-start | bytes 1048576 | tf_op jit(solution)/shard_map/all_to_all | solution.py:214
  203.7 22.6 %all-to-all-done.4 = bf16[16,16,1024]{2,1,0:T(8,128)(2,1)S(1)} async-done(((bf16[16,16,1024]{2,1,0:T(8,128)(2,1)}), bf16[16,16,1024]{2,1,0:T(8,128)(2,1)S(1)}, u32[]{:S(2)}, u32[]{:S(2)}) %all-to-all-start.4) | async-done | bytes 524320 | tf_op jit(solution)/shard_map/all_to_all | solution.py:214
  227.2 1.0 copy.57
  228.2 11.2 %all-to-all-start.5 = ((bf16[32,256,32]{1,2,0:T(8,128)(2,1)}), bf16[32,256,32]{1,2,0:T(8,128)(2,1)}, u32[]{:S(2)}, u32[]{:S(2)}) async-start(bf16[32,256,32]{1,2,0:T(8,128)(2,1)} %bitcast.26), calls=%async_computation.5 | async-start | bytes 1048576 | tf_op jit(solution)/shard_map/all_to_all | solution.py:67
  239.5 2.1 gather_fusion
  241.6 1.1 broadcast_select_fusion
  242.7 8.5 %all-to-all-done.5 = bf16[32,256,32]{1,2,0:T(8,128)(2,1)} async-done(((bf16[32,256,32]{1,2,0:T(8,128)(2,1)}), bf16[32,256,32]{1,2,0:T(8,128)(2,1)}, u32[]{:S(2)}, u32[]{:S(2)}) %all-to-all-start.5) | async-done | bytes 524320 | tf_op jit(solution)/shard_map/all_to_all | solution.py:67
  251.2 3.7 %all-to-all-start.1 = ((bf16[32,16,1024]{2,1,0:T(8,128)(2,1)}), bf16[32,16,1024]{2,1,0:T(8,128)(2,1)S(1)}, u32[]{:S(2)}, u32[]{:S(2)}) async-start(bf16[32,16,1024]{2,1,0:T(8,128)(2,1)} %broadcast_select_fusion), calls=%async_computation.1 | async-start | bytes 2097152 | tf_op jit(solution)/shard_map/all_to_all | solution.py:123
  255.0 3.3 %fusion.8 = (f32[512]{0:T(512)S(1)}, f32[512,1024]{1,0:T(8,128)}) fusion(bf16[512,1024]{1,0:T(8,128)(2,1)S(1)} %get-tuple-element.40, f32[512]{0:T(512)S(1)} %add_rsqrt_fusion, bf16[256,1024]{1,0:T(8,128)(2,1)} %bitcast.22, f32[512,256]{0,1:T(8,128)} %copy-done.10, f32[512]{0:T(512)S(1)} %get-tuple-element.34, f32[512]{0:T(512)S(1)} %fusion.51, ...), kind=kOutput, calls=%fused_computation.22 | convolution fusion | flops 273022464 | bytes 5253120 | tf_op jit(solution)/shard_map/dot_general | solution.py:205
  258.3 1.1 convert_reduce_fusion.1
  259.5 1.1 multiply_reduce_fusion
  260.6 11.1 %all-to-all-done.1 = bf16[32,16,1024]{2,1,0:T(8,128)(2,1)S(1)} async-done(((bf16[32,16,1024]{2,1,0:T(8,128)(2,1)}), bf16[32,16,1024]{2,1,0:T(8,128)(2,1)S(1)}, u32[]{:S(2)}, u32[]{:S(2)}) %all-to-all-start.1) | async-done | bytes 1048608 | tf_op jit(solution)/shard_map/all_to_all | solution.py:123
  272.3 3.9 %all-to-all-start.6 = ((f32[32,1,256]{2,1,0:T(1,128)}), f32[32,1,256]{2,1,0:T(1,128)S(1)}, u32[]{:S(2)}, u32[]{:S(2)}) async-start(f32[32,1,256]{2,1,0:T(1,128)} %broadcast_in_dim.55), calls=%async_computation.6 | async-start | bytes 65536 | tf_op jit(solution)/shard_map/all_to_all | solution.py:50
  276.3 3.0 %fusion.11 = bf16[512,1024]{1,0:T(8,128)(2,1)} fusion(f32[512,1024]{1,0:T(8,128)} %get-tuple-element.44, bf16[512,1024]{1,0:T(8,128)(2,1)S(1)} %get-tuple-element.40, f32[512]{0:T(512)S(1)} %broadcast_multiply_fusion.2, f32[512]{0:T(512)S(1)} %add_rsqrt_fusion), kind=kLoop, calls=%fused_computation.25 | loop fusion | flops 3145728 | bytes 4198400 | tf_op jit(solution)/shard_map/convert_element_type | solution.py:210
  279.3 2.0 gather_fusion.1
  281.2 2.3 all-to-all-done.6
  283.6 1.1 subtract_multiply_fusion
  (87 shorter events, 14.7 us)
Async XLA Ops:
  0.6 28.2 %copy-start = (bf16[512,1024]{1,0:T(8,128)(2,1)S(1)}, bf16[512,1024]{1,0:T(8,128)(2,1)}, u32[]{:S(2)}) copy-start(bf16[512,1024]{1,0:T(8,128)(2,1)} %param.11) | copy-start | bytes 3145732
  0.6 28.6 %copy-start.5 = (s32[512]{0:T(512)S(1)}, s32[512]{0:T(512)}, u32[]{:S(2)}) copy-start(s32[512]{0:T(512)} %param.15) | copy-start | bytes 6148
  0.7 28.7 %copy-start.1 = (bf16[256,1024]{1,0:T(8,128)(2,1)S(1)}, bf16[256,1024]{1,0:T(8,128)(2,1)}, u32[]{:S(2)}) copy-start(bf16[256,1024]{1,0:T(8,128)(2,1)} %param.17) | copy-start | bytes 1572868
  0.7 30.0 %copy-start.4 = (s32[16,256]{1,0:T(8,128)S(1)}, s32[16,256]{1,0:T(8,128)}, u32[]{:S(2)}) copy-start(s32[16,256]{1,0:T(8,128)} %param.16) | copy-start | bytes 49156
  0.7 39.4 %collective-permute-start = (bf16[64,2048]{1,0:T(8,128)(2,1)}, bf16[64,2048]{1,0:T(8,128)(2,1)}, u32[]{:S(2)}, u32[]{:S(2)}) collective-permute-start(bf16[64,2048]{1,0:T(8,128)(2,1)} %param.19), channel_id=1, source_target_pairs={{0,1},{1,2},{2,3},{3,4},{4,5},{5,6},{6,7},{7,8},{8,9},{9,10},{10,1... | collective-permute-start | bytes 786440 | tf_op jit(solution)/shard_map/ppermute | solution.py:27
  5.2 38.1 %collective-permute-start.1 = (bf16[64,2048]{1,0:T(8,128)(2,1)}, bf16[64,2048]{1,0:T(8,128)(2,1)}, u32[]{:S(2)}, u32[]{:S(2)}) collective-permute-start(bf16[64,2048]{1,0:T(8,128)(2,1)} %param.19), channel_id=1, source_target_pairs={{0,15},{1,0},{2,1},{3,2},{4,3},{5,4},{6,5},{7,6},{8,7},{9,8},{10,9... | collective-permute-start | bytes 786440 | tf_op jit(solution)/shard_map/ppermute | solution.py:35
  16.6 124.7 %all-to-all-start = ((bf16[16,512,64]{1,2,0:T(8,128)(2,1)}), bf16[16,512,64]{1,2,0:T(8,128)(2,1)}, u32[]{:S(2)}, u32[]{:S(2)}) async-start(bf16[16,512,64]{1,2,0:T(8,128)(2,1)} %broadcast_in_dim.46), calls=%async_computation | async-start | bytes 2097152 | tf_op jit(solution)/shard_map/all_to_all | solution.py:50
  28.8 5.2 %copy-start.2 = (bf16[64,2048]{1,0:T(8,128)(2,1)S(1)}, bf16[64,2048]{1,0:T(8,128)(2,1)}, u32[]{:S(2)}) copy-start(bf16[64,2048]{1,0:T(8,128)(2,1)} %param.19) | copy-start | bytes 786436
  28.8 5.9 %copy-start.3 = (s32[1,32]{1,0:T(1,128)S(1)}, s32[1,32]{1,0:T(1,128)}, u32[]{:S(2)}) copy-start(s32[1,32]{1,0:T(1,128)} %param.12) | copy-start | bytes 388
  28.8 5.9 %copy-start.6 = (s32[1,32]{1,0:T(1,128)S(1)}, s32[1,32]{1,0:T(1,128)}, u32[]{:S(2)}) copy-start(s32[1,32]{1,0:T(1,128)} %param.14) | copy-start | bytes 388
  28.8 5.9 %copy-start.7 = (s32[1,32]{1,0:T(1,128)S(1)}, s32[1,32]{1,0:T(1,128)}, u32[]{:S(2)}) copy-start(s32[1,32]{1,0:T(1,128)} %param.13) | copy-start | bytes 388
  39.2 92.1 %copy-start.8 = (f32[1024]{0:T(1024)S(1)}, f32[1024]{0:T(1024)}, u32[]{:S(2)}) copy-start(f32[1024]{0:T(1024)} %param.18) | copy-start | bytes 12292
  40.1 38.6 %collective-permute-start.2 = (bf16[64,2048]{1,0:T(8,128)(2,1)}, bf16[64,2048]{1,0:T(8,128)(2,1)S(1)}, u32[]{:S(2)}, u32[]{:S(2)}) collective-permute-start(bf16[64,2048]{1,0:T(8,128)(2,1)} %collective-permute-done), channel_id=1, source_target_pairs={{0,1},{1,2},{2,3},{3,4},{4,5},{5,6},{6,7},{7,8},{8,9},{9,10},{10,1... | collective-permute-start | bytes 786440 | tf_op jit(solution)/shard_map/ppermute | solution.py:27
  43.3 37.2 %collective-permute-start.3 = (bf16[64,2048]{1,0:T(8,128)(2,1)}, bf16[64,2048]{1,0:T(8,128)(2,1)S(1)}, u32[]{:S(2)}, u32[]{:S(2)}) collective-permute-start(bf16[64,2048]{1,0:T(8,128)(2,1)} %collective-permute-done.1), channel_id=1, source_target_pairs={{0,15},{1,0},{2,1},{3,2},{4,3},{5,4},{6,5},{7,6},{8,7},{9,8},{10,9... | collective-permute-start | bytes 786440 | tf_op jit(solution)/shard_map/ppermute | solution.py:35
  78.6 9.6 %collective-permute-start.4 = (bf16[64,2048]{1,0:T(8,128)(2,1)S(1)}, bf16[64,2048]{1,0:T(8,128)(2,1)S(1)}, u32[]{:S(2)}, u32[]{:S(2)}) collective-permute-start(bf16[64,2048]{1,0:T(8,128)(2,1)S(1)} %collective-permute-done.2), channel_id=1, source_target_pairs={{0,1},{1,2},{2,3},{3,4},{4,5},{5,6},{6,7},{7,8},{8,9},{9,10},{10,1... | collective-permute-start | bytes 786440 | tf_op jit(solution)/shard_map/ppermute | solution.py:27
  80.6 9.6 %collective-permute-start.5 = (bf16[64,2048]{1,0:T(8,128)(2,1)S(1)}, bf16[64,2048]{1,0:T(8,128)(2,1)S(1)}, u32[]{:S(2)}, u32[]{:S(2)}) collective-permute-start(bf16[64,2048]{1,0:T(8,128)(2,1)S(1)} %collective-permute-done.3), channel_id=1, source_target_pairs={{0,15},{1,0},{2,1},{3,2},{4,3},{5,4},{6,5},{7,6},{8,7},{9,8},{10,9... | collective-permute-start | bytes 786440 | tf_op jit(solution)/shard_map/ppermute | solution.py:35
  88.2 8.7 %collective-permute-start.6 = (bf16[64,2048]{1,0:T(8,128)(2,1)S(1)}, bf16[64,2048]{1,0:T(8,128)(2,1)S(1)}, u32[]{:S(2)}, u32[]{:S(2)}) collective-permute-start(bf16[64,2048]{1,0:T(8,128)(2,1)S(1)} %collective-permute-done.4), channel_id=1, source_target_pairs={{0,1},{1,2},{2,3},{3,4},{4,5},{5,6},{6,7},{7,8},{8,9},{9,10},{10,1... | collective-permute-start | bytes 786440 | tf_op jit(solution)/shard_map/ppermute | solution.py:27
  90.1 8.7 %collective-permute-start.7 = (bf16[64,2048]{1,0:T(8,128)(2,1)S(1)}, bf16[64,2048]{1,0:T(8,128)(2,1)S(1)}, u32[]{:S(2)}, u32[]{:S(2)}) collective-permute-start(bf16[64,2048]{1,0:T(8,128)(2,1)S(1)} %collective-permute-done.5), channel_id=1, source_target_pairs={{0,15},{1,0},{2,1},{3,2},{4,3},{5,4},{6,5},{7,6},{8,7},{9,8},{10,9... | collective-permute-start | bytes 786440 | tf_op jit(solution)/shard_map/ppermute | solution.py:35
  96.9 8.3 %collective-permute-start.8 = (bf16[64,2048]{1,0:T(8,128)(2,1)S(1)}, bf16[64,2048]{1,0:T(8,128)(2,1)S(1)}, u32[]{:S(2)}, u32[]{:S(2)}) collective-permute-start(bf16[64,2048]{1,0:T(8,128)(2,1)S(1)} %collective-permute-done.6), channel_id=1, source_target_pairs={{0,1},{1,2},{2,3},{3,4},{4,5},{5,6},{6,7},{7,8},{8,9},{9,10},{10,1... | collective-permute-start | bytes 786440 | tf_op jit(solution)/shard_map/ppermute | solution.py:27
  98.8 8.3 %collective-permute-start.9 = (bf16[64,2048]{1,0:T(8,128)(2,1)S(1)}, bf16[64,2048]{1,0:T(8,128)(2,1)S(1)}, u32[]{:S(2)}, u32[]{:S(2)}) collective-permute-start(bf16[64,2048]{1,0:T(8,128)(2,1)S(1)} %collective-permute-done.7), channel_id=1, source_target_pairs={{0,15},{1,0},{2,1},{3,2},{4,3},{5,4},{6,5},{7,6},{8,7},{9,8},{10,9... | collective-permute-start | bytes 786440 | tf_op jit(solution)/shard_map/ppermute | solution.py:35
  105.2 8.3 %collective-permute-start.10 = (bf16[64,2048]{1,0:T(8,128)(2,1)S(1)}, bf16[64,2048]{1,0:T(8,128)(2,1)S(1)}, u32[]{:S(2)}, u32[]{:S(2)}) collective-permute-start(bf16[64,2048]{1,0:T(8,128)(2,1)S(1)} %collective-permute-done.8), channel_id=1, source_target_pairs={{0,1},{1,2},{2,3},{3,4},{4,5},{5,6},{6,7},{7,8},{8,9},{9,10},{10,1... | collective-permute-start | bytes 786440 | tf_op jit(solution)/shard_map/ppermute | solution.py:27
  107.2 8.3 %collective-permute-start.11 = (bf16[64,2048]{1,0:T(8,128)(2,1)S(1)}, bf16[64,2048]{1,0:T(8,128)(2,1)S(1)}, u32[]{:S(2)}, u32[]{:S(2)}) collective-permute-start(bf16[64,2048]{1,0:T(8,128)(2,1)S(1)} %collective-permute-done.9), channel_id=1, source_target_pairs={{0,15},{1,0},{2,1},{3,2},{4,3},{5,4},{6,5},{7,6},{8,7},{9,8},{10,9... | collective-permute-start | bytes 786440 | tf_op jit(solution)/shard_map/ppermute | solution.py:35
  113.6 8.3 %collective-permute-start.12 = (bf16[64,2048]{1,0:T(8,128)(2,1)S(1)}, bf16[64,2048]{1,0:T(8,128)(2,1)S(1)}, u32[]{:S(2)}, u32[]{:S(2)}) collective-permute-start(bf16[64,2048]{1,0:T(8,128)(2,1)S(1)} %collective-permute-done.10), channel_id=1, source_target_pairs={{0,1},{1,2},{2,3},{3,4},{4,5},{5,6},{6,7},{7,8},{8,9},{9,10},{10,1... | collective-permute-start | bytes 786440 | tf_op jit(solution)/shard_map/ppermute | solution.py:27
  115.5 9.0 %collective-permute-start.13 = (bf16[64,2048]{1,0:T(8,128)(2,1)S(1)}, bf16[64,2048]{1,0:T(8,128)(2,1)S(1)}, u32[]{:S(2)}, u32[]{:S(2)}) collective-permute-start(bf16[64,2048]{1,0:T(8,128)(2,1)S(1)} %collective-permute-done.11), channel_id=1, source_target_pairs={{0,15},{1,0},{2,1},{3,2},{4,3},{5,4},{6,5},{7,6},{8,7},{9,8},{10,9... | collective-permute-start | bytes 786440 | tf_op jit(solution)/shard_map/ppermute | solution.py:35
  121.9 8.7 %collective-permute-start.14 = (bf16[64,2048]{1,0:T(8,128)(2,1)S(1)}, bf16[64,2048]{1,0:T(8,128)(2,1)S(1)}, u32[]{:S(2)}, u32[]{:S(2)}) collective-permute-start(bf16[64,2048]{1,0:T(8,128)(2,1)S(1)} %collective-permute-done.12), channel_id=1, source_target_pairs={{0,1},{1,2},{2,3},{3,4},{4,5},{5,6},{6,7},{7,8},{8,9},{9,10},{10,1... | collective-permute-start | bytes 786440 | tf_op jit(solution)/shard_map/ppermute | solution.py:27
  141.3 30.9 %all-to-all-start.3 = ((bf16[16,16,1024]{2,1,0:T(8,128)(2,1)}), bf16[16,16,1024]{2,1,0:T(8,128)(2,1)}, u32[]{:S(2)}, u32[]{:S(2)}) async-start(bf16[16,16,1024]{2,1,0:T(8,128)(2,1)} %bitcast.21), calls=%async_computation.3 | async-start | bytes 1048576 | tf_op jit(solution)/shard_map/all_to_all | solution.py:181
  153.2 4.9 %copy-start.9 = (f32[512]{0:T(512)S(1)}, f32[512]{0:T(512)}, u32[]{:S(2)}) copy-start(f32[512]{0:T(512)} %param.20) | copy-start | bytes 6148
  172.2 24.1 %all-to-all-start.2 = ((s32[32,1,2]{2,1,0:T(1,128)}), s32[32,1,2]{2,1,0:T(1,128)S(1)}, u32[]{:S(2)}, u32[]{:S(2)}) async-start(s32[32,1,2]{2,1,0:T(1,128)} %copy.55), calls=%async_computation.2 | async-start | bytes 32768 | tf_op jit(solution)/shard_map/all_to_all | solution.py:124
  191.1 5.3 %copy-start.10 = (f32[512,256]{0,1:T(8,128)}, f32[512,256]{0,1:T(8,128)S(1)}, u32[]{:S(2)}) copy-start(f32[512,256]{0,1:T(8,128)S(1)} %get-tuple-element.42) | copy-start | bytes 1572868
  196.3 29.9 %all-to-all-start.4 = ((bf16[16,16,1024]{2,1,0:T(8,128)(2,1)}), bf16[16,16,1024]{2,1,0:T(8,128)(2,1)S(1)}, u32[]{:S(2)}, u32[]{:S(2)}) async-start(bf16[16,16,1024]{2,1,0:T(8,128)(2,1)} %bitcast.23), calls=%async_computation.4 | async-start | bytes 1048576 | tf_op jit(solution)/shard_map/all_to_all | solution.py:214
  228.2 23.0 %all-to-all-start.5 = ((bf16[32,256,32]{1,2,0:T(8,128)(2,1)}), bf16[32,256,32]{1,2,0:T(8,128)(2,1)}, u32[]{:S(2)}, u32[]{:S(2)}) async-start(bf16[32,256,32]{1,2,0:T(8,128)(2,1)} %bitcast.26), calls=%async_computation.5 | async-start | bytes 1048576 | tf_op jit(solution)/shard_map/all_to_all | solution.py:67
  251.2 20.5 %all-to-all-start.1 = ((bf16[32,16,1024]{2,1,0:T(8,128)(2,1)}), bf16[32,16,1024]{2,1,0:T(8,128)(2,1)S(1)}, u32[]{:S(2)}, u32[]{:S(2)}) async-start(bf16[32,16,1024]{2,1,0:T(8,128)(2,1)} %broadcast_select_fusion), calls=%async_computation.1 | async-start | bytes 2097152 | tf_op jit(solution)/shard_map/all_to_all | solution.py:123
  272.3 11.2 %all-to-all-start.6 = ((f32[32,1,256]{2,1,0:T(1,128)}), f32[32,1,256]{2,1,0:T(1,128)S(1)}, u32[]{:S(2)}, u32[]{:S(2)}) async-start(f32[32,1,256]{2,1,0:T(1,128)} %broadcast_in_dim.55), calls=%async_computation.6 | async-start | bytes 65536 | tf_op jit(solution)/shard_map/all_to_all | solution.py:50
